TPU v7x, 32 devices: a whole 2x2x4 slice. The times are simulated.
32 devices in a mesh: groups: 2 (over y), blk: 4 (over z), uly: 2 (over x), cfg: 2 (over core).
Axes of the slice: x: 2, y: 2, z: 4, core: 2. Of those that a mesh axis runs over, the one named last changes fastest.
Arguments:
- query_rows: bfloat16 [2, 1024, 1536], P('cfg', ('groups', 'blk', 'uly')), parts along dimension 1, may hold values from -6 to 6
- key_rows: bfloat16 [2, 1024, 1536], P('cfg', ('groups', 'blk', 'uly')), parts along dimension 1, may hold values from -6 to 6
- value_rows: bfloat16 [2, 1024, 1536], P('cfg', ('groups', 'blk', 'uly')), parts along dimension 1, may hold values from -6 to 6
Outputs:
- attended: bfloat16 [2, 1024, 1536], P('cfg', ('groups', 'blk', 'uly')), parts along dimension 1
There are 2 independent parts, one for each index of `groups`. A program takes and returns all parts, laid end to end along the dimension named above; each array names one. Nothing has to cross between parts.
All inputs are finite; a program needn't handle non-finite values.
Results may differ from a plain program's by a relative error of at most 0.0045.
Values may be sent and summed in bfloat16 or wider, within the bound.
A program may use at most 128 MiB of HBM per device.

v0:
```python
import functools
import math

import jax
import jax.numpy as jnp
from jax import lax
from jax.experimental import pallas as pl
from jax.experimental.pallas import tpu as pltpu
from jax.sharding import PartitionSpec as P

HD = 128
MESH = pl.DeviceIdType.MESH


def attend(queries, key_part, value_part):
    query_mat = queries[0, :, 0]
    row_count, head_count, head_size = query_mat.shape
    score_scale = 1.0 / math.sqrt(head_size)
    start_state = (
        jnp.full((head_count, row_count), -1e30, jnp.float32),
        jnp.zeros((head_count, row_count), jnp.float32),
        jnp.zeros((row_count, head_count, head_size), jnp.float32),
    )

    def absorb(state, pieces):
        key_piece = pieces[0][0, :, 0]
        value_piece = pieces[1][0, :, 0]
        scores = (
            jnp.einsum("qhd,khd->hqk", query_mat, key_piece, preferred_element_type=jnp.float32)
            * score_scale
        )
        running, totals, accumulated = state
        new_max = jnp.maximum(running, jnp.max(scores, axis=2))
        weights = jnp.exp(scores - new_max[:, :, None])
        factor = jnp.exp(running - new_max)
        totals = totals * factor + jnp.sum(weights, axis=2)
        probabilities = weights.astype(jnp.bfloat16)
        contrib = jnp.einsum(
            "hqk,khd->qhd", probabilities, value_piece, preferred_element_type=jnp.float32
        )
        accumulated = accumulated * factor.T[:, :, None] + contrib
        return (new_max, totals, accumulated)

    whole_keys, whole_values = (
        lax.all_gather(key_part, "blk", axis=1, tiled=True),
        lax.all_gather(value_part, "blk", axis=1, tiled=True),
    )
    key_count = whole_keys.shape[1]
    block_rows = math.gcd(key_count, 1024)

    def one_block(state, counter):
        offset = counter * block_rows
        key_block = lax.dynamic_slice_in_dim(whole_keys, offset, block_rows, 1)
        value_block = lax.dynamic_slice_in_dim(whole_values, offset, block_rows, 1)
        return (absorb(state, (key_block, value_block)), None)

    result, unused = lax.scan(
        one_block, start_state, jnp.arange(key_count // block_rows, dtype=jnp.int32)
    )
    output = (result[2] / result[1].T[:, :, None]).astype(jnp.bfloat16)
    return output.reshape(1, row_count, 1, head_count, head_size)


def gathered(query_rows, key_rows, value_rows):
    ulysses = lax.axis_size("uly")
    tokens = query_rows.shape[1]
    width = query_rows.shape[2]
    heads_local = width // HD // ulysses

    def moved(array):
        sections = array.reshape(1, tokens, ulysses, heads_local, HD)
        return lax.all_to_all(sections, "uly", split_axis=2, concat_axis=1, tiled=True)

    mixed = attend(moved(query_rows), moved(key_rows), moved(value_rows))
    merged = lax.all_to_all(mixed, "uly", split_axis=1, concat_axis=2, tiled=True)
    return merged.reshape(1, tokens, width)


def head_counts(heads_column, blocks):
    counts = [heads_column // blocks] * blocks
    by_middle = sorted(range(blocks), key=lambda z: (abs(2 * z - (blocks - 1)), z))
    for z in by_middle[: heads_column % blocks]:
        counts[z] += 1
    return counts


def exchange_kernel(
    blocks, ulys, rows, heads, q_ref, k_ref, v_ref, o_ref,
    qb, kb, vb, pb, ob, in_send, in_recv, out_send, out_recv, row_in,
):
    peers = blocks * ulys
    column = heads // ulys
    counts = head_counts(column, blocks)
    starts = [sum(counts[:z]) for z in range(blocks)]
    slots = max(counts)
    z = lax.axis_index("blk")
    x = lax.axis_index("uly")
    me = z * ulys + x
    sources = (q_ref, k_ref, v_ref)
    buffers = (qb, kb, vb)
    fold = (1.0 / math.sqrt(HD)) * math.log2(math.e)
    chunk_rows = ulys * rows

    def first_of(pz):
        first = jnp.int32(0)
        for i in range(blocks):
            first = first + jnp.where(pz > i, counts[i], 0)
        return first

    def holds_at(pz, s):
        has = pz < 0
        for i in range(blocks):
            if counts[i] > s:
                has = jnp.logical_or(has, pz == i)
        return has

    my_head = x * column + first_of(z)
    my_rows = pl.ds(pl.multiple_of(me * rows, rows), rows)
    turn = jnp.where(z < blocks // 2, blocks // 2, 0)

    def piece(t, head):
        return sources[t].at[0, :, pl.ds(pl.multiple_of(head * HD, HD), HD)]

    def copy_to(s, t, pz, px):
        return pltpu.make_async_remote_copy(
            src_ref=piece(t, px * column + first_of(pz) + s),
            dst_ref=buffers[t].at[s, my_rows],
            send_sem=in_send.at[s, t, pz * ulys + px],
            recv_sem=in_recv.at[s, t, me],
            device_id={"blk": pz, "uly": px},
            device_id_type=MESH,
        )

    def send(s, pz, px):
        for t in range(3):
            copy_to(s, t, pz, px).start()

    def token(row, to):
        pl.semaphore_signal(
            row_in.at[row], inc=1, device_id={"blk": to, "uly": x}, device_id_type=MESH
        )

    toward = jnp.where(z < blocks // 2, 1, -1)

    def inside(pz):
        return jnp.logical_and(pz >= 0, pz < blocks)

    def send_inputs():
        def adjacent(side):
            pz = z + side

            @pl.when(inside(pz))
            def _():
                token(z, pz)
                send(0, pz, x)

        adjacent(toward)
        adjacent(-toward)
        for d in range(1, ulys):
            send(0, z, lax.rem(x + d, ulys))

        def further(d, side):
            pz = z + side * d
            onward = z - side

            @pl.when(inside(pz))
            def _():
                pl.semaphore_wait(row_in.at[pz], 1)
                pl.when(inside(onward))(lambda: token(pz, onward))
                for e in range(1, ulys):
                    send(0, pz, lax.rem(x + e, ulys))
                if d > 1:
                    send(0, pz, x)

        for d in range(1, blocks):
            further(d, toward)
            further(d, -toward)
        for s in range(1, slots):
            for i in range(blocks):
                pz = lax.rem(turn + i, blocks)
                for e in range(ulys):
                    px = lax.rem(x + e, ulys)
                    other = jnp.logical_or(pz != z, px != x)
                    pl.when(jnp.logical_and(holds_at(pz, s), other))(
                        functools.partial(send, s, pz, px)
                    )

    barrier = pltpu.get_barrier_semaphore()

    def greet(pz, px):
        pl.semaphore_signal(
            barrier, inc=1, device_id={"blk": pz, "uly": px}, device_id_type=MESH
        )

    pl.when(z > 0)(lambda: greet(z - 1, x))
    pl.when(z < blocks - 1)(lambda: greet(z + 1, x))
    for d in range(1, ulys):
        greet(z, lax.rem(x + d, ulys))
    def own(s):
        for t in range(3):
            pltpu.make_async_copy(
                piece(t, my_head + s), buffers[t].at[s, my_rows], in_recv.at[s, t, me]
            ).start()

    for s in range(slots):
        pl.when(holds_at(z, s))(functools.partial(own, s))
    greeted = (ulys - 1) + jnp.where(z > 0, 1, 0) + jnp.where(z < blocks - 1, 1, 0)
    pl.semaphore_wait(barrier, greeted)

    send_inputs()

    def landed(s, t):
        def one(p, carry):
            block = buffers[t].at[s, pl.ds(pl.multiple_of(p * rows, rows), rows)]
            pltpu.make_async_copy(block, block, in_recv.at[s, t, p]).wait()
            return carry

        lax.fori_loop(0, peers, one, 0)

    def out_copy(s, c, px):
        head = pl.multiple_of((my_head + s) * HD, HD)
        begin = pl.multiple_of((c * ulys + px) * rows, rows)
        return ob.at[s, pl.ds(begin, rows)], o_ref.at[0, :, pl.ds(head, HD)]

    def out_remote(s, c, px):
        src, dst = out_copy(s, c, px)
        return pltpu.make_async_remote_copy(
            src_ref=src, dst_ref=dst,
            send_sem=out_send.at[s, c * ulys + px],
            recv_sem=out_recv.at[my_head + s],
            device_id={"blk": c, "uly": px}, device_id_type=MESH,
        )

    def out_local(s, c, px):
        src, dst = out_copy(s, c, px)
        return pltpu.make_async_copy(src, dst, out_recv.at[my_head + s])

    late = jnp.logical_and(lax.axis_index("cfg") == 1, holds_at(z, slots - 1))

    def send_output(s, c):
        for px in range(ulys):
            mine = jnp.logical_and(c == z, x == px)

            @pl.when(mine)
            def _():
                out_local(s, c, px).start()

            @pl.when(jnp.logical_not(mine))
            def _():
                out_remote(s, c, px).start()

    def send_late():
        for s in range(slots - 1):
            for i in range((blocks + 1) // 2):
                send_output(s, jnp.where(z < blocks // 2, blocks - 1 - i, i))

    def one_slot(s):
        landed(s, 0)
        landed(s, 1)
        totals = []
        for i in range(blocks):
            c = jnp.where(z < blocks // 2, blocks - 1 - i, i)
            span = pl.ds(pl.multiple_of(c * chunk_rows, chunk_rows), chunk_rows)
            scores = lax.dot_general(
                qb[s, span, :], kb[s], (((1,), (1,)), ((), ())),
                preferred_element_type=jnp.float32,
            )
            top = jnp.max(scores, axis=1, keepdims=True)
            weights = jnp.exp2((scores - top) * fold)
            totals.append(jnp.sum(weights, axis=1, keepdims=True))
            pb[span, :] = weights.astype(jnp.bfloat16)
        landed(s, 2)
        if s > 0 and s == slots - 1:
            pl.when(late)(send_late)
        for i in range(blocks):
            c = jnp.where(z < blocks // 2, blocks - 1 - i, i)
            span = pl.ds(pl.multiple_of(c * chunk_rows, chunk_rows), chunk_rows)
            mixed = jnp.dot(pb[span, :], vb[s], preferred_element_type=jnp.float32)
            ob[s, span, :] = (mixed / totals[i]).astype(jnp.bfloat16)
            if s < slots - 1 and 2 * i < blocks:
                pl.when(jnp.logical_not(late))(functools.partial(send_output, s, c))
            else:
                send_output(s, c)

    for s in range(slots):
        if min(counts) > s:
            one_slot(s)
        else:
            pl.when(holds_at(z, s))(functools.partial(one_slot, s))

    def result_landed(head, carry):
        block = o_ref.at[0, :, pl.ds(pl.multiple_of(head * HD, HD), HD)]
        pltpu.make_async_copy(block, block, out_recv.at[head]).wait()
        return carry

    def all_sent(p, carry):
        pz, px = p // ulys, lax.rem(p, ulys)
        for s in range(slots):
            @pl.when(jnp.logical_and(p != me, holds_at(pz, s)))
            def _():
                for t in range(3):
                    copy_to(s, t, pz, px).wait_send()

            @pl.when(jnp.logical_and(p != me, holds_at(z, s)))
            def _():
                out_remote(s, pz, px).wait_send()
        return carry

    lax.fori_loop(0, peers, all_sent, 0)
    lax.fori_loop(0, heads, result_landed, 0)


def exchanged(query_rows, key_rows, value_rows):
    blocks = lax.axis_size("blk")
    ulys = lax.axis_size("uly")
    unused, rows, width = query_rows.shape
    heads = width // HD
    peers = blocks * ulys
    slots = max(head_counts(heads // ulys, blocks))
    total = peers * rows
    return pl.pallas_call(
        functools.partial(exchange_kernel, blocks, ulys, rows, heads),
        out_shape=pltpu.VMEM(query_rows.shape, jnp.bfloat16),
        in_specs=[pl.BlockSpec(memory_space=pl.ANY)] * 3,
        out_specs=pl.BlockSpec(memory_space=pltpu.VMEM),
        scratch_shapes=[
            pltpu.VMEM((slots, total, HD), jnp.bfloat16),
            pltpu.VMEM((slots, total, HD), jnp.bfloat16),
            pltpu.VMEM((slots, total, HD), jnp.bfloat16),
            pltpu.VMEM((total, total), jnp.bfloat16),
            pltpu.VMEM((slots, total, HD), jnp.bfloat16),
            pltpu.SemaphoreType.DMA((slots, 3, peers)),
            pltpu.SemaphoreType.DMA((slots, 3, peers)),
            pltpu.SemaphoreType.DMA((slots, peers)),
            pltpu.SemaphoreType.DMA((heads,)),
            pltpu.SemaphoreType.REGULAR((blocks,)),
        ],
        compiler_params=pltpu.CompilerParams(collective_id=0, has_side_effects=True),
    )(query_rows, key_rows, value_rows)


def local(query_rows, key_rows, value_rows):
    blocks = lax.axis_size("blk")
    ulys = lax.axis_size("uly")
    heads = query_rows.shape[2] // HD
    tokens = query_rows.shape[1] * blocks * ulys
    if heads % ulys == 0 and heads // ulys >= blocks and tokens <= 1024:
        return exchanged(query_rows, key_rows, value_rows)
    return gathered(query_rows, key_rows, value_rows)


def solution(mesh):
    spec = P("cfg", ("groups", "blk", "uly"), None)
    return jax.shard_map(
        local, mesh=mesh, in_specs=(spec, spec, spec), out_specs=spec, check_vma=False
    )
```

profile of v0, /device:TPU:0, one launch (start us, length us, event | category | flops | bytes accessed | tf_op | source)
XLA Modules:
  0.0 26.0 jit_solution(12219629883547340419)
XLA Ops:
  0.0 25.4 %shard_map.37 = bf16[1,64,1536]{2,1,0:T(8,128)(2,1)S(1)} custom-call(bf16[1,64,1536]{2,1,0:T(8,128)(2,1)} %q_ref.1, bf16[1,64,1536]{2,1,0:T(8,128)(2,1)} %k_ref.1, bf16[1,64,1536]{2,1,0:T(8,128)(2,1)} %v_ref.1), custom_call_target="tpu_custom_call" | custom-call | tf_op jit(solution)/shard_map/pallas_call | solution.py:321
  25.4 0.7 %copy.5 = bf16[1,64,1536]{2,1,0:T(8,128)(2,1)} copy(bf16[1,64,1536]{2,1,0:T(8,128)(2,1)S(1)} %shard_map.37) | data formatting | bytes 393216
where the time goes:
time: 26.2 us; the launch traced here: 26 us
  Pallas kernels  25.4 us (97%)
  local copies, waits for them, and re-layouts  0.68 us (3%)
    pallas_call x1, Pallas kernels, exchanged(): pl.pallas_call(functools.partial(exchange_kernel, blocks, ulys, rows, hea...  25.4 us
    unnamed x1, local copies, waits for them, and re-layouts  0.68 us

commit v1 on v0

v1 whole, which is shorter than its diff:
```python
import functools
import math

import jax
import jax.numpy as jnp
from jax import lax
from jax.experimental import pallas as pl
from jax.experimental.pallas import tpu as pltpu
from jax.sharding import PartitionSpec as P

HD = 128
MESH = pl.DeviceIdType.MESH


def attend(queries, key_part, value_part):
    query_mat = queries[0, :, 0]
    row_count, head_count, head_size = query_mat.shape
    score_scale = 1.0 / math.sqrt(head_size)
    start_state = (
        jnp.full((head_count, row_count), -1e30, jnp.float32),
        jnp.zeros((head_count, row_count), jnp.float32),
        jnp.zeros((row_count, head_count, head_size), jnp.float32),
    )

    def absorb(state, pieces):
        key_piece = pieces[0][0, :, 0]
        value_piece = pieces[1][0, :, 0]
        scores = (
            jnp.einsum("qhd,khd->hqk", query_mat, key_piece, preferred_element_type=jnp.float32)
            * score_scale
        )
        running, totals, accumulated = state
        new_max = jnp.maximum(running, jnp.max(scores, axis=2))
        weights = jnp.exp(scores - new_max[:, :, None])
        factor = jnp.exp(running - new_max)
        totals = totals * factor + jnp.sum(weights, axis=2)
        probabilities = weights.astype(jnp.bfloat16)
        contrib = jnp.einsum(
            "hqk,khd->qhd", probabilities, value_piece, preferred_element_type=jnp.float32
        )
        accumulated = accumulated * factor.T[:, :, None] + contrib
        return (new_max, totals, accumulated)

    whole_keys, whole_values = (
        lax.all_gather(key_part, "blk", axis=1, tiled=True),
        lax.all_gather(value_part, "blk", axis=1, tiled=True),
    )
    key_count = whole_keys.shape[1]
    block_rows = math.gcd(key_count, 1024)

    def one_block(state, counter):
        offset = counter * block_rows
        key_block = lax.dynamic_slice_in_dim(whole_keys, offset, block_rows, 1)
        value_block = lax.dynamic_slice_in_dim(whole_values, offset, block_rows, 1)
        return (absorb(state, (key_block, value_block)), None)

    result, unused = lax.scan(
        one_block, start_state, jnp.arange(key_count // block_rows, dtype=jnp.int32)
    )
    output = (result[2] / result[1].T[:, :, None]).astype(jnp.bfloat16)
    return output.reshape(1, row_count, 1, head_count, head_size)


def gathered(query_rows, key_rows, value_rows):
    ulysses = lax.axis_size("uly")
    tokens = query_rows.shape[1]
    width = query_rows.shape[2]
    heads_local = width // HD // ulysses

    def moved(array):
        sections = array.reshape(1, tokens, ulysses, heads_local, HD)
        return lax.all_to_all(sections, "uly", split_axis=2, concat_axis=1, tiled=True)

    mixed = attend(moved(query_rows), moved(key_rows), moved(value_rows))
    merged = lax.all_to_all(mixed, "uly", split_axis=1, concat_axis=2, tiled=True)
    return merged.reshape(1, tokens, width)


def exchange_kernel(
    blocks, ulys, rows, heads, q_ref, k_ref, v_ref, o_ref,
    qb, kb, vb, ob, sb, ib, tb,
    in_send, in_recv, out_send, out_recv, row_in,
):
    half = blocks // 2
    owners = half * ulys
    slots = heads // owners
    near = owners * rows
    z = lax.axis_index("blk")
    x = lax.axis_index("uly")
    me = z * ulys + x
    side = z // half
    rank = lax.rem(me, owners)
    sources = (q_ref, k_ref, v_ref)
    buffers = (qb, kb, vb)
    fold = (1.0 / math.sqrt(HD)) * math.log2(math.e)

    def landing(t, j):
        begin = (me if t == 0 else rank) * rows
        return buffers[t].at[j, pl.ds(pl.multiple_of(begin, rows), rows)]

    def arrival(t, j, cross):
        return in_recv.at[j, 3 if cross else t]

    def piece(t, j, pz, px):
        head = (lax.rem(pz, half) * ulys + px) * slots + j
        return sources[t].at[0, :, pl.ds(pl.multiple_of(head * HD, HD), HD)]

    def send(j, pz, px, cross):
        for t in range(1 if cross else 3):
            pltpu.make_async_remote_copy(
                src_ref=piece(t, j, pz, px),
                dst_ref=landing(t, j),
                send_sem=in_send.at[j, t],
                recv_sem=arrival(t, j, cross),
                device_id={"blk": pz, "uly": px},
                device_id_type=MESH,
            ).start()

    barrier = pltpu.get_barrier_semaphore()

    def greet(pz, px):
        pl.semaphore_signal(
            barrier, inc=1, device_id={"blk": pz, "uly": px}, device_id_type=MESH
        )

    pl.when(z > 0)(lambda: greet(z - 1, x))
    pl.when(z < blocks - 1)(lambda: greet(z + 1, x))
    for d in range(1, ulys):
        greet(z, lax.rem(x + d, ulys))
    for j in range(slots):
        for t in range(3):
            pltpu.make_async_copy(
                piece(t, j, z, x), landing(t, j), arrival(t, j, False)
            ).start()
    greeted = (ulys - 1) + jnp.where(z > 0, 1, 0) + jnp.where(z < blocks - 1, 1, 0)
    pl.semaphore_wait(barrier, greeted)

    def token(row, to):
        pl.semaphore_signal(
            row_in.at[row], inc=1, device_id={"blk": to, "uly": x}, device_id_type=MESH
        )

    def send_inputs(zz):
        toward = 1 if zz < half else -1
        sent = set()

        def crosses(pz):
            return pz // half != zz // half

        def give(j, pz, e):
            if (j, pz, e) not in sent:
                sent.add((j, pz, e))
                send(j, pz, lax.rem(x + e, ulys), crosses(pz))

        def hear(pz):
            pl.semaphore_wait(row_in.at[pz], 1)
            onward = zz - 1 if pz > zz else zz + 1
            if 0 <= onward < blocks:
                token(pz, onward)

        def row(j, pz):
            for e in range(ulys):
                if pz != zz or e:
                    give(j, pz, e)

        beside = [zz + s for s in (toward, -toward) if 0 <= zz + s < blocks]
        for pz in beside:
            token(zz, pz)
        for pz in beside:
            for j in range(min(slots, 2) if crosses(pz) else 1):
                give(j, pz, 0)
        row(0, zz)
        for d in range(1, blocks):
            for s in (toward, -toward):
                pz = zz + s * d
                if 0 <= pz < blocks:
                    hear(pz)
                    row(0, pz)
        away = sorted((pz for pz in range(blocks) if crosses(pz)), key=lambda pz: abs(pz - zz))
        mine = sorted((pz for pz in range(blocks) if not crosses(pz)), key=lambda pz: -abs(pz - zz))
        for j in range(1, slots):
            if j < slots - 1:
                for pz in mine:
                    row(j, pz)
            for pz in away:
                row(j, pz)
            if j == slots - 1:
                for pz in mine:
                    row(j, pz)

    for zz in range(blocks):
        pl.when(z == zz)(functools.partial(send_inputs, zz))

    def await_bytes(ref, sem):
        pltpu.make_async_copy(ref, ref, sem).wait()

    def side_rows(which):
        return pl.ds(pl.multiple_of(which * near, near), near)

    def send_output(j, c, px):
        to = c * ulys + px
        copies = (
            (ob.at[j, pl.ds(pl.multiple_of(to * rows, rows), rows)], ib.at[side, j, rank], 0),
            (sb.at[j, to], tb.at[side, j, rank], 1),
        )
        own = to == me

        @pl.when(own)
        def _():
            for src, dst, t in copies:
                pltpu.make_async_copy(src, dst, out_recv.at[side, j, t]).start()

        @pl.when(jnp.logical_not(own))
        def _():
            for src, dst, t in copies:
                pltpu.make_async_remote_copy(
                    src_ref=src, dst_ref=dst,
                    send_sem=out_send.at[j, t], recv_sem=out_recv.at[side, j, t],
                    device_id={"blk": c, "uly": px}, device_id_type=MESH,
                ).start()

    diagonal = (
        lax.broadcasted_iota(jnp.int32, (rows, HD), 0)
        == lax.broadcasted_iota(jnp.int32, (rows, HD), 1)
    )
    chunk = ulys * rows
    for j in range(slots):
        await_bytes(kb.at[j], in_recv.at[j, 1])
        await_bytes(vb.at[j], in_recv.at[j, 2])
        for i in range(blocks):
            if i == 0:
                await_bytes(qb.at[j, side_rows(1 - side)], in_recv.at[j, 3])
            if i == half:
                await_bytes(qb.at[j, side_rows(side)], in_recv.at[j, 0])
            c = jnp.where(z < half, blocks - 1 - i, i)
            span = pl.ds(pl.multiple_of(c * chunk, chunk), chunk)
            scores = lax.dot_general(
                qb[j, span, :], kb[j], (((1,), (1,)), ((), ())),
                preferred_element_type=jnp.float32,
            )
            top = jnp.max(scores, axis=1, keepdims=True)
            weights = jnp.exp2((scores - top) * fold)
            totals = jnp.sum(weights, axis=1, keepdims=True)
            mixed = jnp.dot(
                weights.astype(jnp.bfloat16), vb[j], preferred_element_type=jnp.float32
            )
            ob[j, span, :] = (mixed / totals).astype(jnp.bfloat16)
            level = top * fold + jnp.log2(totals)
            for px in range(ulys):
                part = level[px * rows:(px + 1) * rows]
                sb[j, c * ulys + px] = jnp.sum(
                    jnp.where(diagonal, part, 0.0), axis=0, keepdims=True
                )
            for px in range(ulys):
                send_output(j, c, px)

    for j in range(slots):
        for s in range(2):
            await_bytes(ib.at[s, j], out_recv.at[s, j, 0])
            await_bytes(tb.at[s, j], out_recv.at[s, j, 1])
        for r in range(owners):
            share = 1.0 / (1.0 + jnp.exp2(tb[1, j, r] - tb[0, j, r]))
            share = jnp.sum(jnp.where(diagonal, share, 0.0), axis=1, keepdims=True)
            first = ib[0, j, r].astype(jnp.float32)
            second = ib[1, j, r].astype(jnp.float32)
            merged = second + share * (first - second)
            o_ref[0, :, pl.ds((r * slots + j) * HD, HD)] = merged.astype(jnp.bfloat16)

    others = blocks * ulys - 1
    for j in range(slots):
        await_bytes(qb.at[j, pl.ds(0, others * rows)], in_send.at[j, 0])
        await_bytes(kb.at[j, pl.ds(0, (owners - 1) * rows)], in_send.at[j, 1])
        await_bytes(vb.at[j, pl.ds(0, (owners - 1) * rows)], in_send.at[j, 2])
        await_bytes(ob.at[j, pl.ds(0, others * rows)], out_send.at[j, 0])
        await_bytes(sb.at[j, pl.ds(0, others)], out_send.at[j, 1])


def exchanged(query_rows, key_rows, value_rows):
    blocks = lax.axis_size("blk")
    ulys = lax.axis_size("uly")
    unused, rows, width = query_rows.shape
    heads = width // HD
    owners = blocks // 2 * ulys
    slots = heads // owners
    total = blocks * ulys * rows
    near = owners * rows
    return pl.pallas_call(
        functools.partial(exchange_kernel, blocks, ulys, rows, heads),
        out_shape=pltpu.VMEM(query_rows.shape, jnp.bfloat16),
        in_specs=[pl.BlockSpec(memory_space=pl.ANY)] * 3,
        out_specs=pl.BlockSpec(memory_space=pltpu.VMEM),
        scratch_shapes=[
            pltpu.VMEM((slots, total, HD), jnp.bfloat16),
            pltpu.VMEM((slots, near, HD), jnp.bfloat16),
            pltpu.VMEM((slots, near, HD), jnp.bfloat16),
            pltpu.VMEM((slots, total, HD), jnp.bfloat16),
            pltpu.VMEM((slots, blocks * ulys, 1, HD), jnp.float32),
            pltpu.VMEM((2, slots, owners, rows, HD), jnp.bfloat16),
            pltpu.VMEM((2, slots, owners, 1, HD), jnp.float32),
            pltpu.SemaphoreType.DMA((slots, 3)),
            pltpu.SemaphoreType.DMA((slots, 4)),
            pltpu.SemaphoreType.DMA((slots, 2)),
            pltpu.SemaphoreType.DMA((2, slots, 2)),
            pltpu.SemaphoreType.REGULAR((blocks,)),
        ],
        compiler_params=pltpu.CompilerParams(collective_id=0, has_side_effects=True),
    )(query_rows, key_rows, value_rows)


def local(query_rows, key_rows, value_rows):
    blocks = lax.axis_size("blk")
    ulys = lax.axis_size("uly")
    rows = query_rows.shape[1]
    heads = query_rows.shape[2] // HD
    tokens = rows * blocks * ulys
    even = blocks % 2 == 0 and heads % (blocks // 2 * ulys) == 0
    if even and tokens <= 1024 and rows <= HD and rows % 16 == 0:
        return exchanged(query_rows, key_rows, value_rows)
    return gathered(query_rows, key_rows, value_rows)


def solution(mesh):
    spec = P("cfg", ("groups", "blk", "uly"), None)
    return jax.shard_map(
        local, mesh=mesh, in_specs=(spec, spec, spec), out_specs=spec, check_vma=False
    )
```

time: 26.2 us -> 26.8 us (1.023)
  Pallas kernels: 25.4 us -> 26 us
    pallas_call x1, Pallas kernels: 25.4 us -> 26 us  [exchanged(): pl.pallas_call(functools.partial(exchange_kernel, blocks, ulys, rows, hea...]
where the time goes in v1:
time: 26.8 us; the launch traced here: 26.7 us
  Pallas kernels  26 us (97%)
  local copies, waits for them, and re-layouts  0.68 us (3%)
    pallas_call x1, Pallas kernels, exchanged(): pl.pallas_call(functools.partial(exchange_kernel, blocks, ulys, rows, hea...  26 us
    unnamed x1, local copies, waits for them, and re-layouts  0.68 us

profile of v1, /device:TPU:0, one launch (start us, length us, event | category | flops | bytes accessed | tf_op | source)
XLA Modules:
  0.0 26.7 jit_solution(8837589140699715684)
XLA Ops:
  0.0 26.0 %shard_map.37 = bf16[1,64,1536]{2,1,0:T(8,128)(2,1)S(1)} custom-call(bf16[1,64,1536]{2,1,0:T(8,128)(2,1)} %q_ref.1, bf16[1,64,1536]{2,1,0:T(8,128)(2,1)} %k_ref.1, bf16[1,64,1536]{2,1,0:T(8,128)(2,1)} %v_ref.1), custom_call_target="tpu_custom_call" | custom-call | tf_op jit(solution)/shard_map/pallas_call | solution.py:287
  26.0 0.7 %copy.5 = bf16[1,64,1536]{2,1,0:T(8,128)(2,1)} copy(bf16[1,64,1536]{2,1,0:T(8,128)(2,1)S(1)} %shard_map.37) | data formatting | bytes 393216

commit v2 on v0

--- a/solution.py
+++ b/solution.py
@@ -140,50 +140,47 @@
             row_in.at[row], inc=1, device_id={"blk": to, "uly": x}, device_id_type=MESH
         )
 
-    toward = jnp.where(z < blocks // 2, 1, -1)
-
-    def inside(pz):
-        return jnp.logical_and(pz >= 0, pz < blocks)
-
-    def send_inputs():
-        def adjacent(side):
-            pz = z + side
-
-            @pl.when(inside(pz))
-            def _():
-                token(z, pz)
-                send(0, pz, x)
-
-        adjacent(toward)
-        adjacent(-toward)
-        for d in range(1, ulys):
-            send(0, z, lax.rem(x + d, ulys))
-
-        def further(d, side):
-            pz = z + side * d
-            onward = z - side
-
-            @pl.when(inside(pz))
-            def _():
-                pl.semaphore_wait(row_in.at[pz], 1)
-                pl.when(inside(onward))(lambda: token(pz, onward))
-                for e in range(1, ulys):
-                    send(0, pz, lax.rem(x + e, ulys))
-                if d > 1:
-                    send(0, pz, x)
-
+    def send_inputs(zz):
+        half = blocks // 2
+        toward = 1 if zz < half else -1
+        sent = set()
+
+        def crosses(pz):
+            return pz // half != zz // half
+
+        def give(s, pz, *turns):
+            for e in turns:
+                if counts[pz] > s and (pz != zz or e) and (s, pz, e) not in sent:
+                    sent.add((s, pz, e))
+                    send(s, pz, lax.rem(x + e, ulys))
+
+        def hear(pz):
+            pl.semaphore_wait(row_in.at[pz], 1)
+            onward = zz - 1 if pz > zz else zz + 1
+            if 0 <= onward < blocks:
+                token(pz, onward)
+
+        every = tuple(range(ulys))
+        beside = [zz + e for e in (toward, -toward) if 0 <= zz + e < blocks]
+        away = sorted((pz for pz in range(blocks) if crosses(pz)), key=lambda pz: -abs(pz - zz))
+        mine = sorted((pz for pz in range(blocks) if not crosses(pz)), key=lambda pz: -abs(pz - zz))
+        for pz in beside:
+            token(zz, pz)
+        for s in range(slots):
+            for pz in beside:
+                give(s, pz, 0)
+        for s in range(slots):
+            give(s, zz, *every)
         for d in range(1, blocks):
-            further(d, toward)
-            further(d, -toward)
-        for s in range(1, slots):
-            for i in range(blocks):
-                pz = lax.rem(turn + i, blocks)
-                for e in range(ulys):
-                    px = lax.rem(x + e, ulys)
-                    other = jnp.logical_or(pz != z, px != x)
-                    pl.when(jnp.logical_and(holds_at(pz, s), other))(
-                        functools.partial(send, s, pz, px)
-                    )
+            for e in (toward, -toward):
+                pz = zz + e * d
+                if 0 <= pz < blocks:
+                    hear(pz)
+                    if crosses(pz):
+                        give(0, pz, *every)
+        for s in range(slots):
+            for pz in away + mine:
+                give(s, pz, *every)
 
     barrier = pltpu.get_barrier_semaphore()
 
@@ -207,7 +204,8 @@
     greeted = (ulys - 1) + jnp.where(z > 0, 1, 0) + jnp.where(z < blocks - 1, 1, 0)
     pl.semaphore_wait(barrier, greeted)
 
-    send_inputs()
+    for zz in range(blocks):
+        pl.when(z == zz)(functools.partial(send_inputs, zz))
 
     def landed(s, t):
         def one(p, carry):

time: 26.2 us -> 25.4 us (0.969)
  Pallas kernels: 25.4 us -> 24.6 us
    pallas_call x1, Pallas kernels: 25.4 us -> 24.6 us  [exchanged(): pl.pallas_call(functools.partial(exchange_kernel, blocks, ulys, rows, hea...]
where the time goes in v2:
time: 25.4 us; the launch traced here: 25.3 us
  Pallas kernels  24.6 us (97%)
  local copies, waits for them, and re-layouts  0.68 us (3%)
    pallas_call x1, Pallas kernels, exchanged(): pl.pallas_call(functools.partial(exchange_kernel, blocks, ulys, rows, hea...  24.6 us
    unnamed x1, local copies, waits for them, and re-layouts  0.68 us

profile of v2, /device:TPU:0, one launch (start us, length us, event | category | flops | bytes accessed | tf_op | source)
XLA Modules:
  0.0 25.3 jit_solution(12738330370454064112)
XLA Ops:
  0.0 24.6 %shard_map.37 = bf16[1,64,1536]{2,1,0:T(8,128)(2,1)S(1)} custom-call(bf16[1,64,1536]{2,1,0:T(8,128)(2,1)} %q_ref.1, bf16[1,64,1536]{2,1,0:T(8,128)(2,1)} %k_ref.1, bf16[1,64,1536]{2,1,0:T(8,128)(2,1)} %v_ref.1), custom_call_target="tpu_custom_call" | custom-call | tf_op jit(solution)/shard_map/pallas_call | solution.py:319
  24.6 0.7 %copy.5 = bf16[1,64,1536]{2,1,0:T(8,128)(2,1)} copy(bf16[1,64,1536]{2,1,0:T(8,128)(2,1)S(1)} %shard_map.37) | data formatting | bytes 393216

commit v3 on v1

v3 whole, which is shorter than its diff:
```python
import functools
import math

import jax
import jax.numpy as jnp
from jax import lax
from jax.experimental import pallas as pl
from jax.experimental.pallas import tpu as pltpu
from jax.sharding import PartitionSpec as P

HD = 128
MESH = pl.DeviceIdType.MESH


def attend(queries, key_part, value_part):
    query_mat = queries[0, :, 0]
    row_count, head_count, head_size = query_mat.shape
    score_scale = 1.0 / math.sqrt(head_size)
    start_state = (
        jnp.full((head_count, row_count), -1e30, jnp.float32),
        jnp.zeros((head_count, row_count), jnp.float32),
        jnp.zeros((row_count, head_count, head_size), jnp.float32),
    )

    def absorb(state, pieces):
        key_piece = pieces[0][0, :, 0]
        value_piece = pieces[1][0, :, 0]
        scores = (
            jnp.einsum("qhd,khd->hqk", query_mat, key_piece, preferred_element_type=jnp.float32)
            * score_scale
        )
        running, totals, accumulated = state
        new_max = jnp.maximum(running, jnp.max(scores, axis=2))
        weights = jnp.exp(scores - new_max[:, :, None])
        factor = jnp.exp(running - new_max)
        totals = totals * factor + jnp.sum(weights, axis=2)
        probabilities = weights.astype(jnp.bfloat16)
        contrib = jnp.einsum(
            "hqk,khd->qhd", probabilities, value_piece, preferred_element_type=jnp.float32
        )
        accumulated = accumulated * factor.T[:, :, None] + contrib
        return (new_max, totals, accumulated)

    whole_keys, whole_values = (
        lax.all_gather(key_part, "blk", axis=1, tiled=True),
        lax.all_gather(value_part, "blk", axis=1, tiled=True),
    )
    key_count = whole_keys.shape[1]
    block_rows = math.gcd(key_count, 1024)

    def one_block(state, counter):
        offset = counter * block_rows
        key_block = lax.dynamic_slice_in_dim(whole_keys, offset, block_rows, 1)
        value_block = lax.dynamic_slice_in_dim(whole_values, offset, block_rows, 1)
        return (absorb(state, (key_block, value_block)), None)

    result, unused = lax.scan(
        one_block, start_state, jnp.arange(key_count // block_rows, dtype=jnp.int32)
    )
    output = (result[2] / result[1].T[:, :, None]).astype(jnp.bfloat16)
    return output.reshape(1, row_count, 1, head_count, head_size)


def gathered(query_rows, key_rows, value_rows):
    ulysses = lax.axis_size("uly")
    tokens = query_rows.shape[1]
    width = query_rows.shape[2]
    heads_local = width // HD // ulysses

    def moved(array):
        sections = array.reshape(1, tokens, ulysses, heads_local, HD)
        return lax.all_to_all(sections, "uly", split_axis=2, concat_axis=1, tiled=True)

    mixed = attend(moved(query_rows), moved(key_rows), moved(value_rows))
    merged = lax.all_to_all(mixed, "uly", split_axis=1, concat_axis=2, tiled=True)
    return merged.reshape(1, tokens, width)


def exchange_kernel(
    blocks, ulys, rows, q_ref, k_ref, v_ref, o_ref,
    qf, kf, vf, of, qs, ks, vs, os, sb, ib, tb,
    in_send, in_recv, out_send, out_recv, row_in,
):
    half = blocks // 2
    owners = half * ulys
    peers = blocks * ulys
    near = owners * rows
    chunk = ulys * rows
    z = lax.axis_index("blk")
    x = lax.axis_index("uly")
    me = z * ulys + x
    side = z // half
    lead = lax.axis_index("cfg") == 0
    rank = lax.rem(me, owners)
    sources = (q_ref, k_ref, v_ref)
    wholes = (qf, kf, vf)
    shared = (qs, ks, vs)
    fold = (1.0 / math.sqrt(HD)) * math.log2(math.e)

    def part(begin, size):
        return pl.ds(pl.multiple_of(begin, size), size)

    def whole_copy(t, to):
        return (
            sources[t].at[0, :, part(to * HD, HD)],
            wholes[t].at[part(me * rows, rows)],
        )

    def shared_copy(t, to):
        begin = (me if t == 0 else rank) * rows
        return (
            sources[t].at[0, :, part((peers + lax.rem(to, owners)) * HD, HD)],
            shared[t].at[part(begin, rows)],
        )

    def remote(copy, sent, landed, pz, px):
        pltpu.make_async_remote_copy(
            src_ref=copy[0], dst_ref=copy[1], send_sem=sent, recv_sem=landed,
            device_id={"blk": pz, "uly": px}, device_id_type=MESH,
        ).start()

    def send(kind, pz, px, crosses):
        to = pz * ulys + px
        for t in range(3):
            if kind == 0:
                remote(whole_copy(t, to), in_send.at[0, t], in_recv.at[t], pz, px)
            elif t == 0 or not crosses:
                landed = in_recv.at[6 if crosses else 3 + t]
                remote(shared_copy(t, to), in_send.at[1, t], landed, pz, px)

    barrier = pltpu.get_barrier_semaphore()

    def greet(pz, px):
        pl.semaphore_signal(
            barrier, inc=1, device_id={"blk": pz, "uly": px}, device_id_type=MESH
        )

    pl.when(z > 0)(lambda: greet(z - 1, x))
    pl.when(z < blocks - 1)(lambda: greet(z + 1, x))
    for d in range(1, ulys):
        greet(z, lax.rem(x + d, ulys))
    for t in range(3):
        pltpu.make_async_copy(*whole_copy(t, me), in_recv.at[t]).start()
        pltpu.make_async_copy(*shared_copy(t, me), in_recv.at[3 + t]).start()
    greeted = (ulys - 1) + jnp.where(z > 0, 1, 0) + jnp.where(z < blocks - 1, 1, 0)
    pl.semaphore_wait(barrier, greeted)

    def token(row, to):
        pl.semaphore_signal(
            row_in.at[row], inc=1, device_id={"blk": to, "uly": x}, device_id_type=MESH
        )

    def send_inputs(zz):
        toward = 1 if zz < half else -1
        sent = set()

        def crosses(pz):
            return pz // half != zz // half

        def give(kind, pz, *turns):
            for e in turns:
                if (pz != zz or e) and (kind, pz, e) not in sent:
                    sent.add((kind, pz, e))
                    send(kind, pz, lax.rem(x + e, ulys), crosses(pz))

        def hear(pz):
            pl.semaphore_wait(row_in.at[pz], 1)
            onward = zz - 1 if pz > zz else zz + 1
            if 0 <= onward < blocks:
                token(pz, onward)

        every = tuple(range(ulys))
        beside = [zz + e for e in (toward, -toward) if 0 <= zz + e < blocks]
        away = sorted((pz for pz in range(blocks) if crosses(pz)), key=lambda pz: -abs(pz - zz))
        mine = sorted((pz for pz in range(blocks) if not crosses(pz)), key=lambda pz: -abs(pz - zz))
        for pz in beside:
            token(zz, pz)
        for kind in range(2):
            for pz in beside:
                give(kind, pz, 0)
        for kind in range(2):
            give(kind, zz, *every)
        for d in range(1, blocks):
            for e in (toward, -toward):
                pz = zz + e * d
                if 0 <= pz < blocks:
                    hear(pz)
                    if crosses(pz):
                        give(0, pz, *every)
        for kind in range(2):
            for pz in away + mine:
                give(kind, pz, *every)

    for zz in range(blocks):
        pl.when(z == zz)(functools.partial(send_inputs, zz))

    def await_bytes(ref, sem):
        pltpu.make_async_copy(ref, ref, sem).wait()

    def row_of(i):
        return jnp.where(z < half, blocks - 1 - i, i)

    def deliver(copies, c, px):
        own = c * ulys + px == me

        @pl.when(own)
        def _():
            for src, dst, sent, landed in copies:
                pltpu.make_async_copy(src, dst, landed).start()

        @pl.when(jnp.logical_not(own))
        def _():
            for src, dst, sent, landed in copies:
                remote((src, dst), sent, landed, c, px)

    def send_whole(i):
        c = row_of(i)
        for px in range(ulys):
            src = of.at[part((c * ulys + px) * rows, rows)]
            dst = o_ref.at[0, :, part(me * HD, HD)]
            deliver(((src, dst, out_send.at[0], out_recv.at[0]),), c, px)

    def send_shared(i):
        c = row_of(i)
        for px in range(ulys):
            to = c * ulys + px
            deliver((
                (os.at[part(to * rows, rows)], ib.at[side, rank], out_send.at[1], out_recv.at[1 + side]),
                (sb.at[to], tb.at[side, rank], out_send.at[2], out_recv.at[3 + side]),
            ), c, px)

    def attention(q, k, v):
        scores = lax.dot_general(
            q, k, (((1,), (1,)), ((), ())), preferred_element_type=jnp.float32
        )
        top = jnp.max(scores, axis=1, keepdims=True)
        weights = jnp.exp2((scores - top) * fold)
        totals = jnp.sum(weights, axis=1, keepdims=True)
        mixed = jnp.dot(weights.astype(jnp.bfloat16), v, preferred_element_type=jnp.float32)
        return (mixed / totals).astype(jnp.bfloat16), top * fold + jnp.log2(totals)

    for t in range(3):
        await_bytes(wholes[t], in_recv.at[t])
    for i in range(blocks):
        span = part(row_of(i) * chunk, chunk)
        of[span, :] = attention(qf[span, :], kf[...], vf[...])[0]
        if i >= half:
            send_whole(i)
        elif i == 0:
            pl.when(lead)(functools.partial(send_whole, i))

    diagonal = (
        lax.broadcasted_iota(jnp.int32, (rows, HD), 0)
        == lax.broadcasted_iota(jnp.int32, (rows, HD), 1)
    )
    await_bytes(ks, in_recv.at[4])
    await_bytes(vs, in_recv.at[5])
    await_bytes(qs.at[part((1 - side) * near, near)], in_recv.at[6])
    for i in range(blocks):
        if i == half:
            await_bytes(qs.at[part(side * near, near)], in_recv.at[3])
        c = row_of(i)
        span = part(c * chunk, chunk)
        mixed, level = attention(qs[span, :], ks[...], vs[...])
        os[span, :] = mixed
        for px in range(ulys):
            sb[c * ulys + px] = jnp.sum(
                jnp.where(diagonal, level[px * rows:(px + 1) * rows], 0.0), axis=0, keepdims=True
            )
        if i == half:
            for k in range(half):
                pl.when(jnp.logical_not(lead))(functools.partial(send_whole, k))
        send_shared(i)
        if i == 0:
            for k in range(1, half):
                pl.when(lead)(functools.partial(send_whole, k))

    for s in range(2):
        await_bytes(ib.at[s], out_recv.at[1 + s])
        await_bytes(tb.at[s], out_recv.at[3 + s])
    for r in range(owners):
        share = 1.0 / (1.0 + jnp.exp2(tb[1, r] - tb[0, r]))
        share = jnp.sum(jnp.where(diagonal, share, 0.0), axis=1, keepdims=True)
        first = ib[0, r].astype(jnp.float32)
        second = ib[1, r].astype(jnp.float32)
        merged = second + share * (first - second)
        o_ref[0, :, pl.ds((peers + r) * HD, HD)] = merged.astype(jnp.bfloat16)
    await_bytes(o_ref.at[0, :, pl.ds(0, peers * HD)], out_recv.at[0])

    for t in range(3):
        await_bytes(wholes[t].at[pl.ds(0, (peers - 1) * rows)], in_send.at[0, t])
        others = (peers if t == 0 else owners) - 1
        await_bytes(shared[t].at[pl.ds(0, others * rows)], in_send.at[1, t])
    await_bytes(of.at[pl.ds(0, (peers - 1) * rows)], out_send.at[0])
    await_bytes(os.at[pl.ds(0, (peers - 1) * rows)], out_send.at[1])
    await_bytes(sb.at[pl.ds(0, peers - 1)], out_send.at[2])


def exchanged(query_rows, key_rows, value_rows):
    blocks = lax.axis_size("blk")
    ulys = lax.axis_size("uly")
    rows = query_rows.shape[1]
    owners = blocks // 2 * ulys
    peers = blocks * ulys
    full = pltpu.VMEM((peers * rows, HD), jnp.bfloat16)
    less = pltpu.VMEM((owners * rows, HD), jnp.bfloat16)
    return pl.pallas_call(
        functools.partial(exchange_kernel, blocks, ulys, rows),
        out_shape=pltpu.VMEM(query_rows.shape, jnp.bfloat16),
        in_specs=[pl.BlockSpec(memory_space=pl.ANY)] * 3,
        out_specs=pl.BlockSpec(memory_space=pltpu.VMEM),
        scratch_shapes=[
            full, full, full, full, full, less, less, full,
            pltpu.VMEM((peers, 1, HD), jnp.float32),
            pltpu.VMEM((2, owners, rows, HD), jnp.bfloat16),
            pltpu.VMEM((2, owners, 1, HD), jnp.float32),
            pltpu.SemaphoreType.DMA((2, 3)),
            pltpu.SemaphoreType.DMA((7,)),
            pltpu.SemaphoreType.DMA((3,)),
            pltpu.SemaphoreType.DMA((5,)),
            pltpu.SemaphoreType.REGULAR((blocks,)),
        ],
        compiler_params=pltpu.CompilerParams(collective_id=0, has_side_effects=True),
    )(query_rows, key_rows, value_rows)


def local(query_rows, key_rows, value_rows):
    blocks = lax.axis_size("blk")
    ulys = lax.axis_size("uly")
    rows = query_rows.shape[1]
    heads = query_rows.shape[2] // HD
    peers = blocks * ulys
    even = blocks % 2 == 0 and 2 * heads == 3 * peers
    if even and rows * peers <= 1024 and rows <= HD and rows % 16 == 0:
        return exchanged(query_rows, key_rows, value_rows)
    return gathered(query_rows, key_rows, value_rows)


def solution(mesh):
    spec = P("cfg", ("groups", "blk", "uly"), None)
    return jax.shard_map(
        local, mesh=mesh, in_specs=(spec, spec, spec), out_specs=spec, check_vma=False
    )
```

time: 26.8 us -> 24.9 us (0.929)
  Pallas kernels: 26 us -> 24.1 us
    pallas_call x1, Pallas kernels: 26 us -> 24.1 us  [exchanged(): pl.pallas_call(functools.partial(exchange_kernel, blocks, ulys, rows), ou...]
where the time goes in v3:
time: 24.9 us; the launch traced here: 24.8 us
  Pallas kernels  24.1 us (97%)
  local copies, waits for them, and re-layouts  0.68 us (3%)
    pallas_call x1, Pallas kernels, exchanged(): pl.pallas_call(functools.partial(exchange_kernel, blocks, ulys, rows), ou...  24.1 us
    unnamed x1, local copies, waits for them, and re-layouts  0.68 us

profile of v3, /device:TPU:0, one launch (start us, length us, event | category | flops | bytes accessed | tf_op | source)
XLA Modules:
  0.0 24.8 jit_solution(12410583635130365067)
XLA Ops:
  0.0 24.1 %shard_map.37 = bf16[1,64,1536]{2,1,0:T(8,128)(2,1)S(1)} custom-call(bf16[1,64,1536]{2,1,0:T(8,128)(2,1)} %q_ref.1, bf16[1,64,1536]{2,1,0:T(8,128)(2,1)} %k_ref.1, bf16[1,64,1536]{2,1,0:T(8,128)(2,1)} %v_ref.1), custom_call_target="tpu_custom_call" | custom-call | tf_op jit(solution)/shard_map/pallas_call | solution.py:307
  24.1 0.7 %copy.5 = bf16[1,64,1536]{2,1,0:T(8,128)(2,1)} copy(bf16[1,64,1536]{2,1,0:T(8,128)(2,1)S(1)} %shard_map.37) | data formatting | bytes 393216

commit v4 on v3

--- a/solution.py
+++ b/solution.py
@@ -185,7 +185,8 @@
                 pz = zz + e * d
                 if 0 <= pz < blocks:
                     hear(pz)
-                    if crosses(pz):
+                    outward = abs(2 * pz - blocks + 1) > abs(2 * zz - blocks + 1)
+                    if crosses(pz) or outward:
                         give(0, pz, *every)
         for kind in range(2):
             for pz in away + mine:

time: 24.9 us -> 24.9 us (level)
  no operation moved by 1% of the time
where the time goes in v4:
time: 24.9 us; the launch traced here: 24.8 us
  Pallas kernels  24.1 us (97%)
  local copies, waits for them, and re-layouts  0.68 us (3%)
    pallas_call x1, Pallas kernels, exchanged(): pl.pallas_call(functools.partial(exchange_kernel, blocks, ulys, rows), ou...  24.1 us
    unnamed x1, local copies, waits for them, and re-layouts  0.68 us

profile of v4, /device:TPU:0, one launch (start us, length us, event | category | flops | bytes accessed | tf_op | source)
XLA Modules:
  0.0 24.8 jit_solution(15043399143418993882)
XLA Ops:
  0.0 24.1 %shard_map.37 = bf16[1,64,1536]{2,1,0:T(8,128)(2,1)S(1)} custom-call(bf16[1,64,1536]{2,1,0:T(8,128)(2,1)} %q_ref.1, bf16[1,64,1536]{2,1,0:T(8,128)(2,1)} %k_ref.1, bf16[1,64,1536]{2,1,0:T(8,128)(2,1)} %v_ref.1), custom_call_target="tpu_custom_call" | custom-call | tf_op jit(solution)/shard_map/pallas_call | solution.py:308
  24.1 0.7 %copy.5 = bf16[1,64,1536]{2,1,0:T(8,128)(2,1)} copy(bf16[1,64,1536]{2,1,0:T(8,128)(2,1)S(1)} %shard_map.37) | data formatting | bytes 393216
